TPU v7x, 32 devices: a whole 2x2x4 slice. The times are simulated.
32 devices in a mesh: seq: 4 (over z), fsdp: 8 (over y, x, core).
Axes of the slice: x: 2, y: 2, z: 4, core: 2. Of those that a mesh axis runs over, the one named last changes fastest.
Arguments:
- tokens: bfloat16 [8, 1024, 768], P('fsdp', 'seq'), may hold values from -12 to 12
- cotangent: bfloat16 [8, 1024, 768], P('fsdp', 'seq'), may hold values from -6 to 6
- lengths: int32 [8], P('fsdp'), may hold values from 128 to 1024, as said below
- w_attn: float32 [4, 768, 768], P(None, 'fsdp', 'seq'), may hold values from -0.8660254 to 0.8660254
- attn_first: float32 [4, 768, 768], P(None, 'fsdp', 'seq'), may hold values from -0.3 to 0.3
- attn_second: float32 [4, 768, 768], P(None, 'fsdp', 'seq'), may hold values from 1e-06 to 0.0001
- w_ffn: float32 [2, 768, 3072], P(None, 'fsdp', 'seq'), may hold values from -0.21650635 to 0.21650635
- ffn_first: float32 [2, 768, 3072], P(None, 'fsdp', 'seq'), may hold values from -0.3 to 0.3
- ffn_second: float32 [2, 768, 3072], P(None, 'fsdp', 'seq'), may hold values from 1e-06 to 0.0001
- vectors: float32 [12, 768], P(None, ('seq', 'fsdp')), may hold values from -1 to 1.5
- vec_first: float32 [12, 768], P(None, ('seq', 'fsdp')), may hold values from -0.3 to 0.3
- vec_second: float32 [12, 768], P(None, ('seq', 'fsdp')), may hold values from 1e-06 to 0.0001
Outputs:
- block_out: bfloat16 [8, 1024, 768], P('fsdp', 'seq')
- input_grad: float32 [8, 1024, 768], P('fsdp', 'seq')
- grad_attn: float32 [4, 768, 768], P(None, 'fsdp', 'seq')
- grad_ffn: float32 [2, 768, 3072], P(None, 'fsdp', 'seq')
- grad_vec: float32 [12, 768], P(None, ('seq', 'fsdp'))
- attn_new: float32 [4, 768, 768], P(None, 'fsdp', 'seq')
- attn_first_new: float32 [4, 768, 768], P(None, 'fsdp', 'seq')
- attn_second_new: float32 [4, 768, 768], P(None, 'fsdp', 'seq')
- ffn_new: float32 [2, 768, 3072], P(None, 'fsdp', 'seq')
- ffn_first_new: float32 [2, 768, 3072], P(None, 'fsdp', 'seq')
- ffn_second_new: float32 [2, 768, 3072], P(None, 'fsdp', 'seq')
- vec_new: float32 [12, 768], P(None, ('seq', 'fsdp'))
- vec_first_new: float32 [12, 768], P(None, ('seq', 'fsdp'))
- vec_second_new: float32 [12, 768], P(None, ('seq', 'fsdp'))
Inputs may be any that keep to these rules, and one draw needn't show every extreme that they name: `lengths`: in every draw one sequence has all 1024 tokens valid and one has 128.
All inputs are finite; a program needn't handle non-finite values.
Results may differ from a plain program's by a relative error of at most 0.011.
The roundings to bfloat16 on the way count: a program that leaves them out, or rounds other values in their place, can miss the bound.
Values may be sent and summed in bfloat16 or wider, within the bound.
No kernel may reach another device: no remote copies, remote signals or barrier semaphores. Data moves between devices by JAX's collectives and lax.ppermute only.
A program may use at most 128 MiB of HBM per device.

v0:
```python
import math
import jax
import jax.numpy as jnp
from jax import lax
from jax.sharding import PartitionSpec as P

HEAD = 64
STEP = 3
EPS_NORM = 1e-12
ADAM_RATE = 0.005
BETA_ONE = 0.9
BETA_TWO = 0.999
ADAM_EPS = 1e-08
WEIGHT_DECAY = 0.01


def layer_norm(values):
    center = values - jnp.mean(values, axis=-1, keepdims=True)
    inv_scale = lax.rsqrt(jnp.mean(center * center, axis=-1, keepdims=True) + EPS_NORM)
    return (center * inv_scale, inv_scale)


def norm_back(grad_normed, normed, inv_scale):
    return inv_scale * (
        grad_normed
        - jnp.mean(grad_normed, axis=-1, keepdims=True)
        - normed * jnp.mean(grad_normed * normed, axis=-1, keepdims=True)
    )


def gelu_pair(preact):
    normal_cdf = 0.5 * (1.0 + jax.scipy.special.erf(preact * (1.0 / math.sqrt(2.0))))
    density = jnp.exp(-0.5 * preact * preact) * (1.0 / math.sqrt(2.0 * math.pi))
    return (preact * normal_cdf, normal_cdf + preact * density)


def dot_right_t(left, right):
    return lax.dot_general(
        left, right, (((1,), (1,)), ((), ())), preferred_element_type=jnp.float32
    )


def head_scores(queries, keys_all, valid_len, head_size):
    row_count = queries.shape[0]
    query_heads = queries.reshape(row_count, -1, head_size)
    key_heads = keys_all.reshape(row_count, -1, head_size)
    scores = jnp.einsum("qhd,khd->hqk", query_heads, key_heads, preferred_element_type=jnp.float32)
    scores = scores * (1.0 / math.sqrt(head_size))
    position = jnp.arange(row_count, dtype=jnp.int32)
    return jnp.where(position[None, None, :] < valid_len, scores, -jnp.inf)


def attention_forward(queries, keys_all, values_all, valid_len, head_size):
    row_count = queries.shape[0]
    scores = head_scores(queries, keys_all, valid_len, head_size)
    log_total = jax.nn.logsumexp(scores, axis=-1)
    attn_probs = jnp.exp(scores - log_total[:, :, None]).astype(jnp.bfloat16)
    value_heads = values_all.reshape(row_count, -1, head_size)
    attn_mixed = jnp.einsum(
        "hqk,khd->qhd", attn_probs, value_heads, preferred_element_type=jnp.float32
    )
    return (attn_mixed.reshape(row_count, -1).astype(jnp.bfloat16), log_total)


def attention_backward(
    queries, keys_all, values_all, attn_mixed, grad_mixed, log_total, valid_len, head_size
):
    row_count = queries.shape[0]
    scale_attn = 1.0 / math.sqrt(head_size)
    scores = head_scores(queries, keys_all, valid_len, head_size)
    probs_full = jnp.exp(scores - log_total[:, :, None])
    attn_probs = probs_full.astype(jnp.bfloat16)
    query_heads = queries.reshape(row_count, -1, head_size)
    key_heads = keys_all.reshape(row_count, -1, head_size)
    value_heads = values_all.reshape(row_count, -1, head_size)
    grad_heads = grad_mixed.reshape(row_count, -1, head_size)
    mixed_heads = attn_mixed.reshape(row_count, -1, head_size)
    row_delta = jnp.sum(grad_heads.astype(jnp.float32) * mixed_heads.astype(jnp.float32), axis=-1).T
    grad_probs = jnp.einsum(
        "qhd,khd->hqk", grad_heads, value_heads, preferred_element_type=jnp.float32
    )
    grad_scores = (probs_full * (grad_probs - row_delta[:, :, None])).astype(jnp.bfloat16)
    grad_query = (
        jnp.einsum("hqk,khd->qhd", grad_scores, key_heads, preferred_element_type=jnp.float32)
        * scale_attn
    ).astype(jnp.bfloat16)
    grad_key = (
        jnp.einsum("hqk,qhd->khd", grad_scores, query_heads, preferred_element_type=jnp.float32)
        * scale_attn
    ).astype(jnp.bfloat16)
    grad_value = jnp.einsum(
        "hqk,qhd->khd", attn_probs, grad_heads, preferred_element_type=jnp.float32
    ).astype(jnp.bfloat16)
    return (
        grad_query.reshape(row_count, -1),
        grad_key.reshape(row_count, -1),
        grad_value.reshape(row_count, -1),
    )


def attend_all(qkv_heads, lengths):

    def forward_sequence(packed):
        return attention_forward(packed[0][:, 0], packed[0][:, 1], packed[0][:, 2], packed[1], HEAD)

    return lax.map(forward_sequence, (qkv_heads, lengths))


def attend_back(qkv_heads, mixed_heads, grad_heads, log_total, lengths):

    def backward_sequence(packed):
        grads = attention_backward(
            packed[0][:, 0],
            packed[0][:, 1],
            packed[0][:, 2],
            packed[1],
            packed[2],
            packed[3],
            packed[4],
            HEAD,
        )
        return jnp.stack(grads, axis=1)

    return lax.map(backward_sequence, (qkv_heads, mixed_heads, grad_heads, log_total, lengths))


def adam_step(parameter, gradient, moment_one, moment_two, decay_rate):
    one_new = BETA_ONE * moment_one + (1.0 - BETA_ONE) * gradient
    two_new = BETA_TWO * moment_two + (1.0 - BETA_TWO) * gradient * gradient
    one_hat = one_new / (1.0 - BETA_ONE**STEP)
    two_hat = two_new / (1.0 - BETA_TWO**STEP)
    update = one_hat / (jnp.sqrt(two_hat) + ADAM_EPS)
    return (parameter - ADAM_RATE * (update + decay_rate * parameter), one_new, two_new)


def on_device(
    tokens,
    cotangent,
    lengths,
    w_attn,
    attn_first,
    attn_second,
    w_ffn,
    ffn_first,
    ffn_second,
    vectors,
    vec_first,
    vec_second,
):
    seq_local, shard_len, model_width = tokens.shape
    row_count = seq_local * shard_len
    attn_rows, ffn_rows = (
        lax.all_gather(w_attn.astype(jnp.bfloat16), "fsdp", axis=1, tiled=True),
        lax.all_gather(w_ffn.astype(jnp.bfloat16), "fsdp", axis=1, tiled=True),
    )
    vec_half = lax.all_gather(vectors.astype(jnp.bfloat16), ("seq", "fsdp"), axis=1, tiled=True)
    vec_wide = lax.optimization_barrier(vec_half).astype(jnp.float32)
    zero_bias = jnp.zeros((model_width,), jnp.float32)
    bias_qkv = jnp.stack([vec_wide[0], zero_bias, vec_wide[1]])
    up_bias = vec_wide[8:12].reshape(-1)
    token_rows = tokens.reshape(row_count, model_width)
    cot_rows = cotangent.reshape(row_count, model_width).astype(jnp.float32)
    attn_w, ffn_w = (
        lax.all_gather(attn_rows, "seq", axis=2, tiled=True),
        lax.all_gather(ffn_rows, "seq", axis=2, tiled=True),
    )
    qkv = (
        jnp.einsum("rd,kde->rke", token_rows, attn_w[:3], preferred_element_type=jnp.float32)
        + bias_qkv
    ).astype(jnp.bfloat16)
    qkv_heads = lax.all_to_all(
        qkv.reshape(seq_local, shard_len, 3, model_width),
        "seq",
        split_axis=3,
        concat_axis=1,
        tiled=True,
    )
    mixed_heads, log_total = attend_all(qkv_heads, lengths)
    mixed_local = lax.all_to_all(mixed_heads, "seq", split_axis=1, concat_axis=2, tiled=True)
    mixed_rows = mixed_local.reshape(row_count, model_width)
    hidden_one = token_rows.astype(jnp.float32) + dot_right_t(mixed_rows, attn_w[3]) + vec_wide[2]
    normed_one, inv_one = layer_norm(hidden_one)
    resid_one = normed_one * vec_wide[4] + vec_wide[5]
    resid_half = resid_one.astype(jnp.bfloat16)
    preact = jnp.dot(resid_half, ffn_w[0], preferred_element_type=jnp.float32) + up_bias
    activation, gelu_slope = gelu_pair(preact)
    act_half = activation.astype(jnp.bfloat16)
    hidden_two = resid_one + dot_right_t(act_half, ffn_w[1]) + vec_wide[3]
    normed_two, inv_two = layer_norm(hidden_two)
    block_out = (normed_two * vec_wide[6] + vec_wide[7]).astype(jnp.bfloat16)
    grad_two = norm_back(cot_rows * vec_wide[6], normed_two, inv_two)
    grad_two_half = grad_two.astype(jnp.bfloat16)
    grad_pre = jnp.dot(grad_two_half, ffn_w[1], preferred_element_type=jnp.float32) * gelu_slope
    grad_pre_half = grad_pre.astype(jnp.bfloat16)
    grad_resid = grad_two + dot_right_t(grad_pre_half, ffn_w[0])
    grad_one = norm_back(grad_resid * vec_wide[4], normed_one, inv_one)
    grad_one_half = grad_one.astype(jnp.bfloat16)
    grad_mixed = jnp.dot(grad_one_half, attn_w[3], preferred_element_type=jnp.float32).astype(
        jnp.bfloat16
    )
    grad_heads = lax.all_to_all(
        grad_mixed.reshape(seq_local, shard_len, model_width),
        "seq",
        split_axis=2,
        concat_axis=1,
        tiled=True,
    )
    grad_stack = attend_back(qkv_heads, mixed_heads, grad_heads, log_total, lengths)
    grad_qkv = lax.all_to_all(grad_stack, "seq", split_axis=1, concat_axis=3, tiled=True).reshape(
        row_count, 3, model_width
    )
    input_grad = grad_one + jnp.einsum(
        "rke,kde->rd", grad_qkv, attn_w[:3], preferred_element_type=jnp.float32
    )
    attn_local = jnp.concatenate(
        [
            jnp.einsum("rd,rke->kde", token_rows, grad_qkv, preferred_element_type=jnp.float32),
            jnp.dot(grad_one_half.T, mixed_rows, preferred_element_type=jnp.float32)[None],
        ],
        axis=0,
    )
    ffn_local = jnp.stack(
        [
            jnp.dot(resid_half.T, grad_pre_half, preferred_element_type=jnp.float32),
            jnp.dot(grad_two_half.T, act_half, preferred_element_type=jnp.float32),
        ]
    )
    qkv_sums = jnp.sum(grad_qkv.astype(jnp.float32), axis=0)
    vec_local = jnp.concatenate(
        [
            jnp.stack(
                [
                    qkv_sums[0],
                    qkv_sums[2],
                    jnp.sum(grad_one, axis=0),
                    jnp.sum(grad_two, axis=0),
                    jnp.sum(grad_resid * normed_one, axis=0),
                    jnp.sum(grad_resid, axis=0),
                    jnp.sum(cot_rows * normed_two, axis=0),
                    jnp.sum(cot_rows, axis=0),
                ]
            ),
            jnp.sum(grad_pre, axis=0).reshape(4, model_width),
        ],
        axis=0,
    )
    attn_part, ffn_part, vec_part = (
        lax.psum_scatter(attn_local, "seq", scatter_dimension=2, tiled=True),
        lax.psum_scatter(ffn_local, "seq", scatter_dimension=2, tiled=True),
        lax.psum_scatter(vec_local, "seq", scatter_dimension=1, tiled=True),
    )
    attn_grad, ffn_grad, vec_grad = (
        lax.psum_scatter(attn_part, "fsdp", scatter_dimension=1, tiled=True),
        lax.psum_scatter(ffn_part, "fsdp", scatter_dimension=1, tiled=True),
        lax.psum_scatter(vec_part, "fsdp", scatter_dimension=1, tiled=True),
    )
    token_total = seq_local * shard_len * lax.axis_size("seq") * lax.axis_size("fsdp")
    grad_scale = float(token_total) ** (-0.5)
    attn_grad = attn_grad * grad_scale
    ffn_grad = ffn_grad * grad_scale
    vec_grad = vec_grad * grad_scale
    attn_new, attn_one, attn_two = adam_step(
        w_attn, attn_grad, attn_first, attn_second, WEIGHT_DECAY
    )
    ffn_new, ffn_one, ffn_two = adam_step(w_ffn, ffn_grad, ffn_first, ffn_second, WEIGHT_DECAY)
    vec_new, vec_one, vec_two = adam_step(vectors, vec_grad, vec_first, vec_second, 0.0)
    return (
        block_out.reshape(seq_local, shard_len, model_width),
        input_grad.reshape(seq_local, shard_len, model_width),
        attn_grad,
        ffn_grad,
        vec_grad,
        attn_new,
        attn_one,
        attn_two,
        ffn_new,
        ffn_one,
        ffn_two,
        vec_new,
        vec_one,
        vec_two,
    )


def solution(mesh):
    placed = (
        P("fsdp", "seq", None),
        P("fsdp", "seq", None),
        P("fsdp"),
        P(None, "fsdp", "seq"),
        P(None, "fsdp", "seq"),
        P(None, "fsdp", "seq"),
        P(None, "fsdp", "seq"),
        P(None, "fsdp", "seq"),
        P(None, "fsdp", "seq"),
        P(None, ("seq", "fsdp")),
        P(None, ("seq", "fsdp")),
        P(None, ("seq", "fsdp")),
    )
    return jax.shard_map(
        on_device,
        mesh=mesh,
        in_specs=placed,
        out_specs=(
            P("fsdp", "seq", None),
            P("fsdp", "seq", None),
            P(None, "fsdp", "seq"),
            P(None, "fsdp", "seq"),
            P(None, ("seq", "fsdp")),
            P(None, "fsdp", "seq"),
            P(None, "fsdp", "seq"),
            P(None, "fsdp", "seq"),
            P(None, "fsdp", "seq"),
            P(None, "fsdp", "seq"),
            P(None, "fsdp", "seq"),
            P(None, ("seq", "fsdp")),
            P(None, ("seq", "fsdp")),
            P(None, ("seq", "fsdp")),
        ),
        check_vma=False,
    )
```

profile of v0, /device:TPU:0, one launch (start us, length us, event | category | flops | bytes accessed | tf_op | source)
XLA Modules:
  0.0 1114.0 jit_solution(3864774587014703365)
XLA Ops:
  11.1 27.6 %all-gather.6.cloned.1.call-done = bf16[4,768,192]{2,0,1:T(4,128)(2,1)} async-done(((bf16[4,96,192]{2,0,1:T(4,128)(2,1)}), bf16[4,768,192]{2,0,1:T(4,128)(2,1)}) %all-gather.6.cloned.1.call-update) | async-done | bytes 1179664 | tf_op jit(solution)/shard_map/all_gather | solution.py:153
  38.8 4.2 copy.151
  43.0 27.2 %all-gather.10.cloned.1.call-done = bf16[2,768,768]{2,1,0:T(8,128)(2,1)} async-done(((bf16[2,96,768]{2,1,0:T(8,128)(2,1)}), bf16[2,768,768]{2,1,0:T(8,128)(2,1)}) %all-gather.10.cloned.1.call-update) | async-done | bytes 2359312 | tf_op jit(solution)/shard_map/all_gather | solution.py:154
  70.2 42.6 %all-gather = bf16[32,24,12]{1,2,0:T(8,128)(2,1)S(1)} all-gather(bf16[1,24,12]{1,2,0:T(8,128)(2,1)S(1)} %convert_bitcast_fusion.1), channel_id=1, replica_groups=mesh['seq'=4,'fsdp'=8] {'seq','fsdp'}, dimensions={0}, use_global_device_ids=true | all-gather | bytes 19008 | tf_op jit(solution)/shard_map/all_gather | solution.py:156
  113.8 47.7 %all-gather.8.cloned.1.call-done = bf16[4,768,768]{1,0,2:T(4,128)(2,1)} async-done(((bf16[4,768,192]{1,0,2:T(4,128)(2,1)}), bf16[4,768,768]{1,0,2:T(4,128)(2,1)}) %all-gather.8.cloned.1.call-update) | async-done | bytes 4718608 | tf_op jit(solution)/shard_map/all_gather | solution.py:164
  161.5 6.5 copy.200
  168.0 3.4 fusion.12
  171.4 3.7 copy.154
  175.1 3.7 all-to-all-start
  179.5 79.6 %all-to-all-done = bf16[1,256,3,768]{1,2,0,3:T(4,128)(2,1)S(1)} async-done(((bf16[1,256,3,768]{1,2,0,3:T(4,128)(2,1)}), bf16[1,256,3,768]{1,2,0,3:T(4,128)(2,1)S(1)}, u32[]{:S(2)}, u32[]{:S(2)}) %all-to-all-start) | async-done | bytes 1179680 | tf_op jit(solution)/shard_map/all_to_all | solution.py:171
  261.1 2.3 fusion.1
  263.5 3.2 exponential_reduce_fusion
  268.0 3.0 fusion
  275.1 4.0 reduce.14
  280.5 3.7 all-to-all-start.1
  284.3 6.2 slice.101
  290.5 5.4 copy.201
  295.9 10.5 all-to-all-done.1
  308.4 2.3 copy.159
  312.9 57.1 %all-gather.12.cloned.1.call-done = bf16[2,768,3072]{2,1,0:T(8,128)(2,1)} async-done(((bf16[2,768,768]{2,1,0:T(8,128)(2,1)}), bf16[2,768,3072]{2,1,0:T(8,128)(2,1)}) %all-gather.12.cloned.1.call-update) | async-done | bytes 9437200 | tf_op jit(solution)/shard_map/all_gather | solution.py:165
  370.0 3.7 multiply_convert_fusion.1
  379.1 2.5 fusion.53
  385.8 2.6 copy.162
  388.4 3.0 reduce.15
  391.5 14.5 %all_to_all.60 = bf16[4,2,24576]{2,1,0:T(2,128)(2,1)S(1)} all-to-all(bf16[4,2,24576]{2,1,0:T(2,128)(2,1)S(1)} %reshape.192), channel_id=1, replica_groups=mesh['seq'=4,'fsdp'=8] {'seq'}, dimensions={0} | all-to-all | bytes 786432 | tf_op jit(solution)/shard_map/all_to_all | solution.py:201
  407.1 5.6 convolution_convert_fusion
  412.9 7.1 multiply_convert_fusion
  420.0 2.8 fusion.20
  425.6 2.4 copy.169
  428.0 3.5 copy.168
  431.5 6.0 maximum_bitcast_fusion
  437.5 3.6 all-to-all-start.3
  441.3 3.0 convolution_bitcast_fusion.3
  444.4 44.5 %all-to-all-done.3 = bf16[1,1024,3,192]{3,2,0,1:T(4,128)(2,1)S(1)} async-done(((bf16[1,1024,3,192]{3,2,0,1:T(4,128)(2,1)}), bf16[1,1024,3,192]{3,2,0,1:T(4,128)(2,1)S(1)}, u32[]{:S(2)}, u32[]{:S(2)}) %all-to-all-start.3) | async-done | bytes 1179680 | tf_op jit(solution)/shard_map/all_to_all | solution.py:209
  490.2 3.9 copy.192
  496.4 4.3 pad_maximum_fusion.1
  501.9 2.9 convolution_bitcast_fusion
  506.4 7.0 pad_maximum_fusion
  516.7 144.4 %reduce-scatter.11.cloned.1.call-done = f32[4,768,192]{1,2,0:T(8,128)} async-done(((f32[4,768,768]{1,2,0:T(8,128)}), f32[4,768,192]{1,2,0:T(8,128)}) %reduce-scatter.11.cloned.1.call-update) | async-done | bytes 2359312 | tf_op jit(solution)/shard_map/reduce_scatter | solution.py:248
  661.1 3.1 copy.193
  664.2 3.1 reshape.176
  667.4 310.8 %reduce-scatter.13.cloned.1.call-done = f32[2,768,768]{2,1,0:T(8,128)} async-done(((f32[2,768,3072]{2,1,0:T(8,128)}), f32[2,768,768]{2,1,0:T(8,128)}) %reduce-scatter.13.cloned.1.call-update) | async-done | bytes 4718608 | tf_op jit(solution)/shard_map/reduce_scatter | solution.py:249
  980.2 4.0 fusion.18
  984.2 18.7 %reduce-scatter.19.cloned.1.call-done = f32[192,12]{1,0:T(8,128)} async-done(((f32[768,12]{1,0:T(8,128)}), f32[192,12]{1,0:T(8,128)}) %reduce-scatter.19.cloned.1.call-update) | async-done | bytes 9232
  1003.9 22.3 %all-reduce = f32[12,192]{1,0:T(8,128)S(1)} all-reduce(f32[12,192]{1,0:T(8,128)S(1)} %copy.196), channel_id=7, replica_groups=mesh['seq'=4,'fsdp'=8] {'fsdp'}, use_global_device_ids=true, to_apply=%region_24.25.clone | all-reduce | flops 2304 | bytes 18432
  1026.9 20.0 %reduce-scatter.17.cloned.1.call-done = f32[96,768]{1,0:T(8,128)} async-done(((f32[768,768]{1,0:T(8,128)}), f32[96,768]{1,0:T(8,128)}) %reduce-scatter.17.cloned.1.call-update) | async-done | bytes 294928
  1054.2 49.9 %reduce-scatter.15.cloned.1.call-done = f32[2,96,768]{2,1,0:T(8,128)} async-done(((f32[2,768,768]{2,1,0:T(8,128)}), f32[2,96,768]{2,1,0:T(8,128)}) %reduce-scatter.15.cloned.1.call-update) | async-done | bytes 589840 | tf_op jit(solution)/shard_map/reduce_scatter | solution.py:254
  1104.1 3.2 multiply_subtract_fusion
  (166 shorter events, 51.3 us)
Async XLA Ops:
  7.2 31.6 %all-gather.6.cloned.1.call-start = ((), (), s32[]{:S(2)}) async-start(), calls=%async_computation.9 | async-start | bytes 1769472 | tf_op jit(solution)/shard_map/all_gather | solution.py:153
  9.2 61.0 %copy-start.28 = (f32[12,24]{1,0:T(8,128)S(1)}, f32[12,24]{1,0:T(8,128)}, u32[]{:S(2)}) copy-start(f32[12,24]{1,0:T(8,128)} %param.21) | copy-start | bytes 3460
  9.2 61.0 %all-gather.10.cloned.1.call-start = ((), (), s32[]{:S(2)}) async-start(), calls=%async_computation.11 | async-start | bytes 2654208 | tf_op jit(solution)/shard_map/all_gather | solution.py:154
  11.1 150.4 %all-gather.8.cloned.1.call-start = ((), (), s32[]{:S(2)}) async-start(), calls=%async_computation.10 | async-start | bytes 5898240 | tf_op jit(solution)/shard_map/all_gather | solution.py:164
  43.0 327.1 %all-gather.12.cloned.1.call-start = ((), (), s32[]{:S(2)}) async-start(), calls=%async_computation.12 | async-start | bytes 11796480 | tf_op jit(solution)/shard_map/all_gather | solution.py:165
  113.0 48.4 %copy-start.26 = (bf16[768,12]{0,1:T(8,128)(2,1)}, bf16[768,12]{0,1:T(8,128)(2,1)S(1)}, u32[]{:S(2)}) copy-start(bf16[768,12]{0,1:T(8,128)(2,1)S(1)} %reshape.173) | copy-start | bytes 55300
  168.0 7.1 copy-start.12
  175.1 84.0 %all-to-all-start = ((bf16[1,256,3,768]{1,2,0,3:T(4,128)(2,1)}), bf16[1,256,3,768]{1,2,0,3:T(4,128)(2,1)S(1)}, u32[]{:S(2)}, u32[]{:S(2)}) async-start(bf16[1,256,3,768]{1,2,0,3:T(4,128)(2,1)} %copy.154), calls=%async_computation | async-start | bytes 3145728 | tf_op jit(solution)/shard_map/all_to_all | solution.py:171
  261.1 9.9 copy-start.17
  263.5 4.6 copy-start
  271.0 2.7 copy-start.1
  273.7 10.6 copy-start.10
  273.7 10.4 copy-start.27
  280.5 26.0 %all-to-all-start.1 = ((bf16[4,2,24576]{2,1,0:T(2,128)(2,1)}), bf16[4,2,24576]{2,1,0:T(2,128)(2,1)S(1)}, u32[]{:S(2)}, u32[]{:S(2)}) async-start(bf16[4,2,24576]{2,1,0:T(2,128)(2,1)} %reshape.190), calls=%async_computation.1 | async-start | bytes 786432 | tf_op jit(solution)/shard_map/all_to_all | solution.py:179
  370.0 5.7 copy-start.31
  373.8 3.5 copy-start.21
  375.7 1.8 copy-start.8
  379.1 2.5 copy-start.13
  381.6 1.7 copy-start.22
  383.6 0.9 copy-start.4
  407.1 5.7 copy-start.11
  407.1 5.8 copy-start.18
  422.7 2.0 copy-start.20
  437.5 51.4 %all-to-all-start.3 = ((bf16[1,1024,3,192]{3,2,0,1:T(4,128)(2,1)}), bf16[1,1024,3,192]{3,2,0,1:T(4,128)(2,1)S(1)}, u32[]{:S(2)}, u32[]{:S(2)}) async-start(bf16[1,1024,3,192]{3,2,0,1:T(4,128)(2,1)} %maximum_bitcast_fusion), calls=%async_computation.3 | async-start | bytes 4194304 | tf_op jit(solution)/shard_map/all_to_all | solution.py:209
  441.1 220.0 %reduce-scatter.11.cloned.1.call-start = ((), (), s32[]{:S(2)}) async-start(), calls=%async_computation.13 | async-start | bytes 11796480 | tf_op jit(solution)/shard_map/reduce_scatter | solution.py:248
  444.4 49.9 %copy-start.16 = (bf16[1,256,768]{2,1,0:T(8,128)(2,1)S(1)}, bf16[1,256,768]{2,1,0:T(8,128)(2,1)}, u32[]{:S(2)}) copy-start(bf16[1,256,768]{2,1,0:T(8,128)(2,1)} %param.12) | copy-start | bytes 1179652
  488.9 1.3 copy-start.3
  494.3 1.1 copy-start.6
  494.3 2.1 copy-start.2
  500.7 1.1 copy-start.14
  500.7 477.5 %reduce-scatter.13.cloned.1.call-start = ((), (), s32[]{:S(2)}) async-start(), calls=%async_computation.14 | async-start | bytes 23592960 | tf_op jit(solution)/shard_map/reduce_scatter | solution.py:249
  501.9 3.0 copy-start.23
  513.4 1.0 copy-start.9
  513.4 489.5 %reduce-scatter.19.cloned.1.call-start = ((), (), s32[]{:S(2)}) async-start(), calls=%async_computation.17 | async-start | bytes 491520
  516.6 530.3 %reduce-scatter.17.cloned.1.call-start = ((), (), s32[]{:S(2)}) async-start(), calls=%async_computation.16 | async-start | bytes 2654208
  667.4 310.9 %copy-start.19 = (f32[4,96,192]{2,1,0:T(8,128)S(1)}, f32[4,96,192]{2,1,0:T(8,128)}, u32[]{:S(2)}) copy-start(f32[4,96,192]{2,1,0:T(8,128)} %param.15) | copy-start | bytes 884740
  667.4 311.1 %copy-start.24 = (f32[4,96,192]{2,1,0:T(8,128)S(1)}, f32[4,96,192]{2,1,0:T(8,128)}, u32[]{:S(2)}) copy-start(f32[4,96,192]{2,1,0:T(8,128)} %param.16) | copy-start | bytes 884740
  667.4 311.3 %copy-start.25 = (f32[4,96,192]{2,1,0:T(8,128)S(1)}, f32[4,96,192]{2,1,0:T(8,128)}, u32[]{:S(2)}) copy-start(f32[4,96,192]{2,1,0:T(8,128)} %param.17) | copy-start | bytes 884740
  667.4 436.7 %reduce-scatter.15.cloned.1.call-start = ((), (), s32[]{:S(2)}) async-start(), calls=%async_computation.15 | async-start | bytes 5308416 | tf_op jit(solution)/shard_map/reduce_scatter | solution.py:254
  978.3 0.7 copy-start.32
  978.3 1.9 copy-start.5
  978.3 1.9 copy-start.7
  978.9 47.3 %copy-start.29 = (f32[12,24]{1,0:T(8,128)S(1)}, f32[12,24]{1,0:T(8,128)}, u32[]{:S(2)}) copy-start(f32[12,24]{1,0:T(8,128)} %param.22) | copy-start | bytes 3460
  978.9 47.3 %copy-start.30 = (f32[12,24]{1,0:T(8,128)S(1)}, f32[12,24]{1,0:T(8,128)}, u32[]{:S(2)}) copy-start(f32[12,24]{1,0:T(8,128)} %param.23) | copy-start | bytes 3460
  1048.2 55.9 %copy-start.15 = (f32[2,96,768]{2,1,0:T(8,128)S(1)}, f32[2,96,768]{2,1,0:T(8,128)}, u32[]{:S(2)}) copy-start(f32[2,96,768]{2,1,0:T(8,128)} %param.18) | copy-start | bytes 1769476
Sparse Core Ops, SparseCore 0:
  10.4 28.2 all-gather.5
  41.2 28.8 all-gather.9
  71.7 89.6 all-gather.7
  162.9 207.1 all-gather.11
  500.9 160.2 reduce-scatter.10
  663.3 314.8 reduce-scatter.12
  981.1 21.7 reduce-scatter.18
  1006.2 40.6 reduce-scatter.16
  1050.4 53.6 reduce-scatter.14
where the time goes:
time: 1120 us; the launch traced here: 1110 us
  waiting for transfers between devices  838 us (75%)
  blocking collectives  79.5 us (7%)
  local copies, waits for them, and re-layouts  78.1 us (7%)
  matrix products  49.4 us (4%)
  other arithmetic  41.2 us (4%)
  between operations  16.1 us (1%)
  starting transfers between devices  11.6 us (1%)
    reduce_scatter x1, waiting for transfers between devices, on_device(): lax.psum_scatter(ffn_local, 'seq', scatter_dimension=2, tiled=True)  311 us
    reduce_scatter x1, waiting for transfers between devices, on_device(): lax.psum_scatter(attn_local, 'seq', scatter_dimension=2, tiled=True)  144 us
    all_to_all x1, waiting for transfers between devices, on_device(): lax.all_to_all(qkv.reshape(seq_local, shard_len, 3, model_width), 'seq',...  79.6 us
    all_gather x1, waiting for transfers between devices, on_device(): lax.all_gather(ffn_rows, 'seq', axis=2, tiled=True)  57.1 us
    reduce_scatter x1, waiting for transfers between devices, on_device(): lax.psum_scatter(ffn_part, 'fsdp', scatter_dimension=1, tiled=True)  49.9 us
    all_gather x1, waiting for transfers between devices, on_device(): lax.all_gather(attn_rows, 'seq', axis=2, tiled=True)  47.7 us
    all_to_all x1, waiting for transfers between devices, on_device(): lax.all_to_all(grad_stack, 'seq', split_axis=1, concat_axis=3, tiled=True)  44.5 us
    unnamed x90, local copies, waits for them, and re-layouts  43.9 us
  transfers between devices with their start and end apart: 12, of which 12 were waited for; matrix products, arithmetic and copies ran while one was open for 8% of the time, Pallas kernels for 0%

commit v1 on v0

--- a/solution.py
+++ b/solution.py
@@ -168,12 +168,18 @@
         jnp.einsum("rd,kde->rke", token_rows, attn_w[:3], preferred_element_type=jnp.float32)
         + bias_qkv
     ).astype(jnp.bfloat16)
-    qkv_heads = lax.all_to_all(
-        qkv.reshape(seq_local, shard_len, 3, model_width),
-        "seq",
-        split_axis=3,
-        concat_axis=1,
-        tiled=True,
+    qkv_heads = jnp.concatenate(
+        lax.all_to_all(
+            jnp.stack(
+                jnp.split(
+                    qkv.reshape(seq_local, shard_len, 3, model_width), lax.axis_size("seq"), axis=3
+                )
+            ),
+            "seq",
+            0,
+            0,
+        ),
+        axis=1,
     )
     mixed_heads, log_total = attend_all(qkv_heads, lengths)
     mixed_local = lax.all_to_all(mixed_heads, "seq", split_axis=1, concat_axis=2, tiled=True)

time: 1120 us -> 1110 us (level)
    all_to_all x1, waiting for transfers between devices: 79.6 us -> 61.9 us  [on_device(): lax.all_to_all(jnp.stack(jnp.split(qkv.reshape(seq_local, shard_len, 3, m...]
    unnamed x90 -> x94, local copies, waits for them, and re-layouts: 43.9 us -> 44.5 us
where the time goes in v1:
time: 1110 us
  waiting for transfers between devices  832 us (75%)
  blocking collectives  79.5 us (7%)
  local copies, waits for them, and re-layouts  76.7 us (7%)
  matrix products  48.4 us (4%)
  other arithmetic  41.2 us (4%)
  between operations  16.1 us (1%)
  starting transfers between devices  11.5 us (1%)
    reduce_scatter x1, waiting for transfers between devices, on_device(): lax.psum_scatter(ffn_local, 'seq', scatter_dimension=2, tiled=True)  311 us
    reduce_scatter x1, waiting for transfers between devices, on_device(): lax.psum_scatter(attn_local, 'seq', scatter_dimension=2, tiled=True)  144 us
    all_gather x1, waiting for transfers between devices, on_device(): lax.all_gather(ffn_rows, 'seq', axis=2, tiled=True)  67.9 us
    all_to_all x1, waiting for transfers between devices, on_device(): lax.all_to_all(jnp.stack(jnp.split(qkv.reshape(seq_local, shard_len, 3, m...  61.9 us
    reduce_scatter x1, waiting for transfers between devices, on_device(): lax.psum_scatter(ffn_part, 'fsdp', scatter_dimension=1, tiled=True)  49.8 us
    all_gather x1, waiting for transfers between devices, on_device(): lax.all_gather(attn_rows, 'seq', axis=2, tiled=True)  47.7 us
    unnamed x94, local copies, waits for them, and re-layouts  44.5 us
    all_to_all x1, waiting for transfers between devices, on_device(): lax.all_to_all(grad_stack, 'seq', split_axis=1, concat_axis=3, tiled=True)  44.5 us
  transfers between devices with their start and end apart: 12, of which 12 were waited for; matrix products, arithmetic and copies ran while one was open for 8% of the time, Pallas kernels for 0%

profile of v1, /device:TPU:0, one launch (start us, length us, event | category | flops | bytes accessed | tf_op | source)
XLA Modules:
  0.0 1105.3 jit_solution(16055257712252431222)
XLA Ops:
  11.1 27.6 %all-gather.6.cloned.1.call-done = bf16[4,768,192]{2,0,1:T(4,128)(2,1)} async-done(((bf16[4,96,192]{2,0,1:T(4,128)(2,1)}), bf16[4,768,192]{2,0,1:T(4,128)(2,1)}) %all-gather.6.cloned.1.call-update) | async-done | bytes 1179664 | tf_op jit(solution)/shard_map/all_gather | solution.py:153
  38.8 4.2 copy.147
  43.0 27.2 %all-gather.10.cloned.1.call-done = bf16[2,768,768]{2,1,0:T(8,128)(2,1)} async-done(((bf16[2,96,768]{2,1,0:T(8,128)(2,1)}), bf16[2,768,768]{2,1,0:T(8,128)(2,1)}) %all-gather.10.cloned.1.call-update) | async-done | bytes 2359312 | tf_op jit(solution)/shard_map/all_gather | solution.py:154
  70.2 42.6 %all-gather = bf16[32,24,12]{1,2,0:T(8,128)(2,1)S(1)} all-gather(bf16[1,24,12]{1,2,0:T(8,128)(2,1)S(1)} %convert_bitcast_fusion.1), channel_id=1, replica_groups=mesh['seq'=4,'fsdp'=8] {'seq','fsdp'}, dimensions={0}, use_global_device_ids=true | all-gather | bytes 19008 | tf_op jit(solution)/shard_map/all_gather | solution.py:156
  113.8 47.7 %all-gather.8.cloned.1.call-done = bf16[4,768,768]{1,0,2:T(4,128)(2,1)} async-done(((bf16[4,768,192]{1,0,2:T(4,128)(2,1)}), bf16[4,768,768]{1,0,2:T(4,128)(2,1)}) %all-gather.8.cloned.1.call-update) | async-done | bytes 4718608 | tf_op jit(solution)/shard_map/all_gather | solution.py:164
  161.5 6.5 copy.195
  168.0 2.4 fusion.12
  172.7 3.7 all-to-all-start
  177.1 61.9 %all-to-all-done = bf16[4,1,256,3,192]{2,4,3,1,0:T(8,128)(2,1)S(1)} async-done(((bf16[4,1,256,3,192]{2,4,3,1,0:T(8,128)(2,1)}), bf16[4,1,256,3,192]{2,4,3,1,0:T(8,128)(2,1)S(1)}, u32[]{:S(2)}, u32[]{:S(2)}) %all-to-all-start) | async-done | bytes 1179680 | tf_op jit(solution)/shard_map/all_to_all | solution.py:172
  240.8 2.3 fusion.1
  243.2 3.2 exponential_reduce_fusion
  247.7 3.0 fusion
  254.8 4.0 reduce.14
  260.2 3.7 all-to-all-start.1
  264.0 6.2 slice.101
  270.2 5.4 copy.196
  275.7 11.7 %all-to-all-done.1 = bf16[4,2,24576]{2,1,0:T(2,128)(2,1)S(1)} async-done(((bf16[4,2,24576]{2,1,0:T(2,128)(2,1)}), bf16[4,2,24576]{2,1,0:T(2,128)(2,1)S(1)}, u32[]{:S(2)}, u32[]{:S(2)}) %all-to-all-start.1) | async-done | bytes 393248 | tf_op jit(solution)/shard_map/all_to_all | solution.py:185
  289.3 2.3 copy.154
  293.8 67.9 %all-gather.12.cloned.1.call-done = bf16[2,768,3072]{2,1,0:T(8,128)(2,1)} async-done(((bf16[2,768,768]{2,1,0:T(8,128)(2,1)}), bf16[2,768,3072]{2,1,0:T(8,128)(2,1)}) %all-gather.12.cloned.1.call-update) | async-done | bytes 9437200 | tf_op jit(solution)/shard_map/all_gather | solution.py:165
  361.7 3.7 multiply_convert_fusion.1
  370.8 2.5 fusion.53
  377.5 2.6 copy.157
  380.1 3.0 reduce.15
  383.2 14.5 %all_to_all.50 = bf16[4,2,24576]{2,1,0:T(2,128)(2,1)S(1)} all-to-all(bf16[4,2,24576]{2,1,0:T(2,128)(2,1)S(1)} %reshape.193), channel_id=1, replica_groups=mesh['seq'=4,'fsdp'=8] {'seq'}, dimensions={0} | all-to-all | bytes 786432 | tf_op jit(solution)/shard_map/all_to_all | solution.py:207
  398.8 5.6 convolution_convert_fusion
  404.6 7.1 multiply_convert_fusion
  411.7 2.8 fusion.20
  417.3 2.4 copy.164
  419.7 3.5 copy.163
  423.2 6.0 maximum_bitcast_fusion
  429.2 3.6 all-to-all-start.3
  433.1 3.0 convolution_bitcast_fusion.3
  436.1 44.5 %all-to-all-done.3 = bf16[1,1024,3,192]{3,2,0,1:T(4,128)(2,1)S(1)} async-done(((bf16[1,1024,3,192]{3,2,0,1:T(4,128)(2,1)}), bf16[1,1024,3,192]{3,2,0,1:T(4,128)(2,1)S(1)}, u32[]{:S(2)}, u32[]{:S(2)}) %all-to-all-start.3) | async-done | bytes 1179680 | tf_op jit(solution)/shard_map/all_to_all | solution.py:215
  481.9 3.9 copy.187
  488.1 4.3 pad_maximum_fusion.1
  493.6 2.9 convolution_bitcast_fusion
  498.1 7.0 pad_maximum_fusion
  508.4 144.4 %reduce-scatter.11.cloned.1.call-done = f32[4,768,192]{1,2,0:T(8,128)} async-done(((f32[4,768,768]{1,2,0:T(8,128)}), f32[4,768,192]{1,2,0:T(8,128)}) %reduce-scatter.11.cloned.1.call-update) | async-done | bytes 2359312 | tf_op jit(solution)/shard_map/reduce_scatter | solution.py:254
  652.8 3.1 copy.188
  655.9 3.1 reshape.177
  659.2 310.8 %reduce-scatter.13.cloned.1.call-done = f32[2,768,768]{2,1,0:T(8,128)} async-done(((f32[2,768,3072]{2,1,0:T(8,128)}), f32[2,768,768]{2,1,0:T(8,128)}) %reduce-scatter.13.cloned.1.call-update) | async-done | bytes 4718608 | tf_op jit(solution)/shard_map/reduce_scatter | solution.py:255
  972.5 4.0 fusion.18
  976.5 18.1 %reduce-scatter.19.cloned.1.call-done = f32[192,12]{1,0:T(8,128)} async-done(((f32[768,12]{1,0:T(8,128)}), f32[192,12]{1,0:T(8,128)}) %reduce-scatter.19.cloned.1.call-update) | async-done | bytes 9232
  995.6 22.3 %all-reduce = f32[12,192]{1,0:T(8,128)S(1)} all-reduce(f32[12,192]{1,0:T(8,128)S(1)} %copy.191), channel_id=7, replica_groups=mesh['seq'=4,'fsdp'=8] {'fsdp'}, use_global_device_ids=true, to_apply=%region_24.25.clone | all-reduce | flops 2304 | bytes 18432
  1018.6 20.0 %reduce-scatter.17.cloned.1.call-done = f32[96,768]{1,0:T(8,128)} async-done(((f32[768,768]{1,0:T(8,128)}), f32[96,768]{1,0:T(8,128)}) %reduce-scatter.17.cloned.1.call-update) | async-done | bytes 294928
  1041.1 2.0 copy.176
  1046.0 49.8 %reduce-scatter.15.cloned.1.call-done = f32[2,96,768]{2,1,0:T(8,128)} async-done(((f32[2,768,768]{2,1,0:T(8,128)}), f32[2,96,768]{2,1,0:T(8,128)}) %reduce-scatter.15.cloned.1.call-update) | async-done | bytes 589840 | tf_op jit(solution)/shard_map/reduce_scatter | solution.py:260
  1095.8 2.8 multiply_subtract_fusion
  (171 shorter events, 52.0 us)
Async XLA Ops:
  7.2 31.6 %all-gather.6.cloned.1.call-start = ((), (), s32[]{:S(2)}) async-start(), calls=%async_computation.9 | async-start | bytes 1769472 | tf_op jit(solution)/shard_map/all_gather | solution.py:153
  9.2 61.0 %all-gather.10.cloned.1.call-start = ((), (), s32[]{:S(2)}) async-start(), calls=%async_computation.11 | async-start | bytes 2654208 | tf_op jit(solution)/shard_map/all_gather | solution.py:154
  11.1 59.1 %copy-start.30 = (f32[12,24]{1,0:T(8,128)S(1)}, f32[12,24]{1,0:T(8,128)}, u32[]{:S(2)}) copy-start(f32[12,24]{1,0:T(8,128)} %param.21) | copy-start | bytes 3460
  11.1 150.4 %all-gather.8.cloned.1.call-start = ((), (), s32[]{:S(2)}) async-start(), calls=%async_computation.10 | async-start | bytes 5898240 | tf_op jit(solution)/shard_map/all_gather | solution.py:164
  43.0 318.8 %all-gather.12.cloned.1.call-start = ((), (), s32[]{:S(2)}) async-start(), calls=%async_computation.12 | async-start | bytes 11796480 | tf_op jit(solution)/shard_map/all_gather | solution.py:165
  113.0 48.4 %copy-start.28 = (bf16[768,12]{0,1:T(8,128)(2,1)}, bf16[768,12]{0,1:T(8,128)(2,1)S(1)}, u32[]{:S(2)}) copy-start(bf16[768,12]{0,1:T(8,128)(2,1)S(1)} %reshape.174) | copy-start | bytes 55300
  168.0 2.4 copy-start.12
  172.7 66.3 %all-to-all-start = ((bf16[4,1,256,3,192]{2,4,3,1,0:T(8,128)(2,1)}), bf16[4,1,256,3,192]{2,4,3,1,0:T(8,128)(2,1)S(1)}, u32[]{:S(2)}, u32[]{:S(2)}) async-start(bf16[4,1,256,3,192]{2,4,3,1,0:T(8,128)(2,1)} %copy.150), calls=%async_computation | async-start | bytes 2359296 | tf_op jit(solution)/shard_map/all_to_all | solution.py:172
  240.8 9.9 copy-start.17
  243.2 4.6 copy-start
  250.8 2.7 copy-start.1
  253.5 10.6 copy-start.10
  253.5 10.4 copy-start.29
  260.2 27.2 %all-to-all-start.1 = ((bf16[4,2,24576]{2,1,0:T(2,128)(2,1)}), bf16[4,2,24576]{2,1,0:T(2,128)(2,1)S(1)}, u32[]{:S(2)}, u32[]{:S(2)}) async-start(bf16[4,2,24576]{2,1,0:T(2,128)(2,1)} %reshape.191), calls=%async_computation.1 | async-start | bytes 786432 | tf_op jit(solution)/shard_map/all_to_all | solution.py:185
  361.7 5.7 copy-start.33
  365.5 3.5 copy-start.21
  367.4 1.8 copy-start.8
  370.8 2.5 copy-start.13
  373.3 1.7 copy-start.22
  375.3 0.9 copy-start.4
  398.8 5.7 copy-start.11
  398.8 5.8 copy-start.18
  414.4 2.0 copy-start.20
  429.2 51.4 %all-to-all-start.3 = ((bf16[1,1024,3,192]{3,2,0,1:T(4,128)(2,1)}), bf16[1,1024,3,192]{3,2,0,1:T(4,128)(2,1)S(1)}, u32[]{:S(2)}, u32[]{:S(2)}) async-start(bf16[1,1024,3,192]{3,2,0,1:T(4,128)(2,1)} %maximum_bitcast_fusion), calls=%async_computation.3 | async-start | bytes 4194304 | tf_op jit(solution)/shard_map/all_to_all | solution.py:215
  432.8 220.0 %reduce-scatter.11.cloned.1.call-start = ((), (), s32[]{:S(2)}) async-start(), calls=%async_computation.13 | async-start | bytes 11796480 | tf_op jit(solution)/shard_map/reduce_scatter | solution.py:254
  436.1 49.9 %copy-start.16 = (bf16[1,256,768]{2,1,0:T(8,128)(2,1)S(1)}, bf16[1,256,768]{2,1,0:T(8,128)(2,1)}, u32[]{:S(2)}) copy-start(bf16[1,256,768]{2,1,0:T(8,128)(2,1)} %param.12) | copy-start | bytes 1179652
  480.6 1.3 copy-start.3
  486.0 1.1 copy-start.6
  486.0 2.1 copy-start.2
  492.4 1.1 copy-start.14
  492.5 477.5 %reduce-scatter.13.cloned.1.call-start = ((), (), s32[]{:S(2)}) async-start(), calls=%async_computation.14 | async-start | bytes 23592960 | tf_op jit(solution)/shard_map/reduce_scatter | solution.py:255
  493.6 3.0 copy-start.23
  505.1 1.0 copy-start.9
  505.1 489.5 %reduce-scatter.19.cloned.1.call-start = ((), (), s32[]{:S(2)}) async-start(), calls=%async_computation.17 | async-start | bytes 491520
  508.3 530.2 %reduce-scatter.17.cloned.1.call-start = ((), (), s32[]{:S(2)}) async-start(), calls=%async_computation.16 | async-start | bytes 2654208
  659.1 310.9 %copy-start.19 = (f32[4,96,192]{2,1,0:T(8,128)S(1)}, f32[4,96,192]{2,1,0:T(8,128)}, u32[]{:S(2)}) copy-start(f32[4,96,192]{2,1,0:T(8,128)} %param.15) | copy-start | bytes 884740
  659.1 311.1 %copy-start.26 = (f32[4,96,192]{2,1,0:T(8,128)S(1)}, f32[4,96,192]{2,1,0:T(8,128)}, u32[]{:S(2)}) copy-start(f32[4,96,192]{2,1,0:T(8,128)} %param.16) | copy-start | bytes 884740
  659.1 436.7 %reduce-scatter.15.cloned.1.call-start = ((), (), s32[]{:S(2)}) async-start(), calls=%async_computation.15 | async-start | bytes 5308416 | tf_op jit(solution)/shard_map/reduce_scatter | solution.py:260
  970.0 1.0 copy-start.27
  970.0 1.2 copy-start.34
  970.0 2.4 copy-start.5
  970.0 2.4 copy-start.7
  972.4 45.5 %copy-start.31 = (f32[12,24]{1,0:T(8,128)S(1)}, f32[12,24]{1,0:T(8,128)}, u32[]{:S(2)}) copy-start(f32[12,24]{1,0:T(8,128)} %param.22) | copy-start | bytes 3460
  972.4 45.4 %copy-start.32 = (f32[12,24]{1,0:T(8,128)S(1)}, f32[12,24]{1,0:T(8,128)}, u32[]{:S(2)}) copy-start(f32[12,24]{1,0:T(8,128)} %param.23) | copy-start | bytes 3460
  1040.0 55.7 %copy-start.15 = (f32[2,96,768]{2,1,0:T(8,128)S(1)}, f32[2,96,768]{2,1,0:T(8,128)}, u32[]{:S(2)}) copy-start(f32[2,96,768]{2,1,0:T(8,128)} %param.18) | copy-start | bytes 1769476
  1041.1 54.7 %copy-start.24 = (f32[2,96,768]{2,1,0:T(8,128)S(1)}, f32[2,96,768]{2,1,0:T(8,128)}, u32[]{:S(2)}) copy-start(f32[2,96,768]{2,1,0:T(8,128)} %param.19) | copy-start | bytes 1769476
  1041.1 54.7 %copy-start.25 = (f32[2,96,768]{2,1,0:T(8,128)S(1)}, f32[2,96,768]{2,1,0:T(8,128)}, u32[]{:S(2)}) copy-start(f32[2,96,768]{2,1,0:T(8,128)} %param.20) | copy-start | bytes 1769476
Sparse Core Ops, SparseCore 0:
  10.4 28.2 all-gather.5
  41.2 28.8 all-gather.9
  71.7 89.6 all-gather.7
  162.9 198.8 all-gather.11
  492.6 160.2 reduce-scatter.10
  655.1 314.8 reduce-scatter.12
  972.8 21.7 reduce-scatter.18
  997.9 40.5 reduce-scatter.16
  1042.0 53.7 reduce-scatter.14
